TPU v7x, 32 devices: a whole 2x2x4 slice. The times are simulated.
32 devices in a mesh: batch: 8 (over z, y), head: 4 (over x, core).
Axes of the slice: x: 2, y: 2, z: 4, core: 2. Of those that a mesh axis runs over, the one named last changes fastest.
Arguments:
- tokens_in: bfloat16 [32768, 768], P(('batch', 'head')), may hold values from -5.6 to 5.6
- doc_ids: int32 [32768], P('batch'), may hold values from 0 to 3, as said below
- landmark_ids: int32 [32768], P('batch'), may hold values from 0 to 63, as said below
- pad_mask: int32 [32768], P('batch'), may hold values from 0 to 1, as said below
- w_query: bfloat16 [768, 768], P(None, 'head'), may hold values from -0.21875 to 0.21875
- w_key: bfloat16 [768, 768], P(None, 'head'), may hold values from -0.21875 to 0.21875
- w_value: bfloat16 [768, 768], P(None, 'head'), may hold values from -0.21875 to 0.21875
- w_output: bfloat16 [768, 768], P('head'), may hold values from -0.625 to 0.625
- conv_weight: bfloat16 [12, 33], P('head'), may hold values from -0.47851562 to 0.47851562
- first_gain: float32 [768], replicated, may hold values from 0.5 to 1.5
- first_bias: float32 [768], replicated, may hold values from -1.2 to 1.2
- w_inner: bfloat16 [768, 3072], replicated, may hold values from -0.21875 to 0.21875
- w_outer: bfloat16 [3072, 768], replicated, may hold values from -0.109375 to 0.109375
- second_gain: float32 [768], replicated, may hold values from 0.5 to 1.5
- second_bias: float32 [768], replicated, may hold values from -1.2 to 1.2
- out_grad: bfloat16 [32768, 768], P(('batch', 'head')), may hold values from -6 to 6
Outputs:
- layer_out: bfloat16 [32768, 768], P(('batch', 'head'))
- input_grad: bfloat16 [32768, 768], P(('batch', 'head'))
- grad_query: float32 [768, 768], P(None, 'head')
- grad_key: float32 [768, 768], P(None, 'head')
- grad_value: float32 [768, 768], P(None, 'head')
- grad_output: float32 [768, 768], P('head')
- grad_conv: float32 [12, 33], P('head')
- grad_first_gain: float32 [768], replicated
- grad_first_bias: float32 [768], replicated
- grad_inner: float32 [768, 3072], P(None, 'head')
- grad_outer: float32 [3072, 768], P('head')
- grad_second_gain: float32 [768], replicated
- grad_second_bias: float32 [768], replicated
Inputs may be any that keep to these rules, and one draw needn't show every extreme that they name: `doc_ids`: within a row of 4096 tokens document numbers never fall, and each document has 128 real tokens or more. `landmark_ids`: within a document landmark numbers never fall, and every landmark of every document has 2 or more real tokens. `pad_mask`: the padding of a row is its last tokens, at least one, and counts to its last document.
All inputs are finite; a program needn't handle non-finite values.
Results may differ from a plain program's by a relative error of at most 0.018.
Values may be sent and summed in bfloat16 or wider, within the bound.
No kernel may reach another device: no remote copies, remote signals or barrier semaphores. Data moves between devices by JAX's collectives and lax.ppermute only.
A program may use at most 256 MiB of HBM per device.

v0:
```python
import jax
import jax.numpy as jnp
from jax import lax
from jax.sharding import PartitionSpec as P

LAND = 64
KW = 33
HEAD_DIM = 64
NEWTON = 6
DOCS = 4
EXACT_PRECISION = lax.Precision.HIGHEST
NEG_FILL = -1e30
NORM_EPS = 1e-05


def newton_inverse(kernel):
    square_sum = jnp.sum(kernel * kernel, axis=(-2, -1), keepdims=True)
    estimate = jnp.swapaxes(kernel, -1, -2) / square_sum
    identity = jnp.eye(kernel.shape[-1], dtype=kernel.dtype)
    for step_count in range(NEWTON):
        product = jnp.matmul(kernel, estimate, precision=EXACT_PRECISION)
        factor_term = 7.0 * identity - product
        factor_term = 15.0 * identity - jnp.matmul(product, factor_term, precision=EXACT_PRECISION)
        factor_term = 13.0 * identity - jnp.matmul(product, factor_term, precision=EXACT_PRECISION)
        estimate = 0.25 * jnp.matmul(estimate, factor_term, precision=EXACT_PRECISION)
    return estimate


def norm_forward(hidden, scale_vec, shift_vec):
    center = hidden - jnp.mean(hidden, axis=-1, keepdims=True)
    inv_spread = lax.rsqrt(jnp.mean(center * center, axis=-1, keepdims=True) + NORM_EPS)
    normed = center * inv_spread
    return (normed * scale_vec + shift_vec, normed, inv_spread)


def norm_backward(upstream, normed, inv_spread, scale_vec):
    scaled = upstream * scale_vec
    result_grad = inv_spread * (
        scaled
        - jnp.mean(scaled, axis=-1, keepdims=True)
        - normed * jnp.mean(scaled * normed, axis=-1, keepdims=True)
    )
    return (result_grad, jnp.sum(upstream * normed, axis=0), jnp.sum(upstream, axis=0))


def exact_gelu(inputs):
    return jax.nn.gelu(inputs, approximate=False)


def softmax_back(prob_rows, upstream):
    return prob_rows * (upstream - jnp.sum(upstream * prob_rows, axis=-1, keepdims=True))


def shards(
    tokens_in,
    doc_ids,
    landmark_ids,
    pad_mask,
    w_query,
    w_key,
    w_value,
    w_output,
    conv_weight,
    first_gain,
    first_bias,
    w_inner,
    w_outer,
    second_gain,
    second_bias,
    out_grad,
):
    all_tokens = lax.all_gather(tokens_in, "head", axis=0, tiled=True)
    row_len = all_tokens.shape[0]
    local_heads = w_query.shape[1] // HEAD_DIM
    qk_scale = HEAD_DIM ** (-0.25)
    real_rows = pad_mask > 0
    real_float = real_rows.astype(jnp.float32)

    def project(weight, factor):
        mapped = jnp.dot(all_tokens, weight, preferred_element_type=jnp.float32) * factor
        return mapped.astype(jnp.bfloat16).reshape(row_len, local_heads, HEAD_DIM)

    queries = project(w_query, qk_scale)
    key_rows = project(w_key, qk_scale)
    values = project(w_value, 1.0)
    land_total = DOCS * LAND
    columns = jnp.arange(land_total, dtype=jnp.int32)
    segment = doc_ids * LAND + landmark_ids
    member = jnp.logical_and(segment[:, None] == columns[None, :], real_rows[:, None])
    member_float = member.astype(jnp.float32)
    member_low = member.astype(jnp.bfloat16)
    counts = jnp.sum(member_float, axis=0)
    same_doc = doc_ids[:, None] == (columns // LAND)[None, :]
    key_valid = jnp.logical_and(same_doc, real_rows[:, None])

    def landmark_mean(rows_in):
        summed_rows = jnp.einsum(
            "ts,thd->shd", member_low, rows_in, preferred_element_type=jnp.float32
        )
        return (summed_rows / counts[:, None, None]).astype(jnp.bfloat16)

    land_query = landmark_mean(queries)
    land_key = landmark_mean(key_rows)

    def first_scores():
        raw_scores = jnp.einsum(
            "thd,shd->hts", queries, land_key, preferred_element_type=jnp.float32
        )
        return jnp.where(same_doc[None], raw_scores, NEG_FILL)

    def third_scores():
        raw_scores = jnp.einsum(
            "shd,thd->hst", land_query, key_rows, preferred_element_type=jnp.float32
        )
        return jnp.where(key_valid.T[None], raw_scores, NEG_FILL)

    scores_now = first_scores()
    first_lse = jax.nn.logsumexp(scores_now, axis=-1, keepdims=True)
    first_low = jnp.exp(scores_now - first_lse).astype(jnp.bfloat16)
    scores_now = third_scores()
    third_lse = jax.nn.logsumexp(scores_now, axis=-1, keepdims=True)
    third_low = jnp.exp(scores_now - third_lse).astype(jnp.bfloat16)
    carried = jnp.einsum("hst,thd->hsd", third_low, values, preferred_element_type=jnp.float32)

    def small_kernel(land_q, land_k):
        doc_q = land_q.reshape(DOCS, LAND, local_heads, HEAD_DIM)
        doc_k = land_k.reshape(DOCS, LAND, local_heads, HEAD_DIM)
        small_scores = jnp.einsum("aihd,ajhd->haij", doc_q, doc_k, precision=EXACT_PRECISION)
        return newton_inverse(jax.nn.softmax(small_scores, axis=-1))

    inverse, inverse_pull = jax.vjp(
        small_kernel, land_query.astype(jnp.float32), land_key.astype(jnp.float32)
    )
    carried_docs = carried.reshape(local_heads, DOCS, LAND, HEAD_DIM)
    mixed_low = jnp.einsum("haij,hajd->haid", inverse, carried_docs, precision=EXACT_PRECISION)
    mixed_low = mixed_low.reshape(local_heads, land_total, HEAD_DIM).astype(jnp.bfloat16)
    attention = jnp.einsum("hts,hsd->thd", first_low, mixed_low, preferred_element_type=jnp.float32)
    half_width = KW // 2
    conv_float = conv_weight.astype(jnp.float32)
    padded_values = jnp.pad(values.astype(jnp.float32), ((half_width, half_width), (0, 0), (0, 0)))
    padded_docs = jnp.pad(doc_ids, (half_width, half_width), constant_values=-1)
    padded_real = jnp.pad(real_float, (half_width, half_width))
    valid_list = []
    conv_out = jnp.zeros(attention.shape, jnp.float32)
    for offset in range(KW):
        is_valid = jnp.where(
            padded_docs[offset : offset + row_len] == doc_ids,
            padded_real[offset : offset + row_len],
            0.0,
        )
        valid_list.append(is_valid)
        conv_out = conv_out + conv_float[:, offset][None, :, None] * (
            padded_values[offset : offset + row_len] * is_valid[:, None, None]
        )
    heads_out = ((attention + conv_out) * real_float[:, None, None]).astype(jnp.bfloat16)
    heads_out = heads_out.reshape(row_len, local_heads * HEAD_DIM)
    projected = lax.psum_scatter(
        jnp.dot(heads_out, w_output, preferred_element_type=jnp.float32).astype(jnp.bfloat16),
        "head",
        scatter_dimension=0,
        tiled=True,
    ).astype(jnp.float32)
    first_out, first_normed, first_inv = norm_forward(
        tokens_in.astype(jnp.float32) + projected, first_gain, first_bias
    )
    norm_low = first_out.astype(jnp.bfloat16)
    inner_pre = jnp.dot(norm_low, w_inner, preferred_element_type=jnp.float32)
    gelu_values, gelu_pull = jax.vjp(exact_gelu, inner_pre)
    inner_act = gelu_values.astype(jnp.bfloat16)
    outer_out = jnp.dot(inner_act, w_outer, preferred_element_type=jnp.float32)
    second_out, second_normed, second_inv = norm_forward(
        first_out + outer_out, second_gain, second_bias
    )
    layer_out = second_out.astype(jnp.bfloat16)
    second_grad, grad_second_gain, grad_second_bias = norm_backward(
        out_grad.astype(jnp.float32), second_normed, second_inv, second_gain
    )
    outer_low = second_grad.astype(jnp.bfloat16)
    act_grad = jnp.einsum("td,fd->tf", outer_low, w_outer, preferred_element_type=jnp.float32)
    pre_low = gelu_pull(act_grad)[0].astype(jnp.bfloat16)
    first_grad = second_grad + jnp.einsum(
        "tf,df->td", pre_low, w_inner, preferred_element_type=jnp.float32
    )
    first_in_grad, grad_first_gain, grad_first_bias = norm_backward(
        first_grad, first_normed, first_inv, first_gain
    )
    full_inner = jnp.einsum("td,tf->df", norm_low, pre_low, preferred_element_type=jnp.float32)
    full_outer = jnp.einsum("tf,td->fd", inner_act, outer_low, preferred_element_type=jnp.float32)
    grad_inner, grad_outer = (
        lax.psum_scatter(
            full_inner.astype(jnp.bfloat16), "head", scatter_dimension=1, tiled=True
        ).astype(jnp.float32),
        lax.psum_scatter(
            full_outer.astype(jnp.bfloat16), "head", scatter_dimension=0, tiled=True
        ).astype(jnp.float32),
    )
    proj_all = lax.all_gather(first_in_grad.astype(jnp.bfloat16), "head", axis=0, tiled=True)
    grad_output = jnp.einsum("tc,td->cd", heads_out, proj_all, preferred_element_type=jnp.float32)
    heads_grad = jnp.einsum("td,cd->tc", proj_all, w_output, preferred_element_type=jnp.float32)
    heads_grad = heads_grad.astype(jnp.bfloat16).reshape(row_len, local_heads, HEAD_DIM)
    heads_grad = jnp.where(real_rows[:, None, None], heads_grad, jnp.zeros_like(heads_grad))
    mixed_grad = jnp.einsum(
        "hts,thd->hsd", first_low, heads_grad, preferred_element_type=jnp.float32
    )
    first_prob = jnp.exp(first_scores() - first_lse)
    first_weight_grad = jnp.einsum(
        "thd,hsd->hts", heads_grad, mixed_low, preferred_element_type=jnp.float32
    )
    first_score_grad = softmax_back(first_prob, first_weight_grad).astype(jnp.bfloat16)
    grad_queries = jnp.einsum(
        "hts,shd->thd", first_score_grad, land_key, preferred_element_type=jnp.float32
    )
    land_key_grad = jnp.einsum(
        "hts,thd->shd", first_score_grad, queries, preferred_element_type=jnp.float32
    )
    mixed_docs = mixed_grad.reshape(local_heads, DOCS, LAND, HEAD_DIM)
    inverse_grad = jnp.einsum(
        "haid,hajd->haij", mixed_docs, carried_docs, precision=EXACT_PRECISION
    )
    carried_low = jnp.einsum("haij,haid->hajd", inverse, mixed_docs, precision=EXACT_PRECISION)
    carried_low = carried_low.reshape(local_heads, land_total, HEAD_DIM).astype(jnp.bfloat16)
    third_prob = jnp.exp(third_scores() - third_lse)
    third_weight_grad = jnp.einsum(
        "hsd,thd->hst", carried_low, values, preferred_element_type=jnp.float32
    )
    third_score_grad = softmax_back(third_prob, third_weight_grad).astype(jnp.bfloat16)
    land_query_grad = jnp.einsum(
        "hst,thd->shd", third_score_grad, key_rows, preferred_element_type=jnp.float32
    )
    grad_keys = jnp.einsum(
        "hst,shd->thd", third_score_grad, land_query, preferred_element_type=jnp.float32
    )
    grad_values = jnp.einsum(
        "hst,hsd->thd", third_low, carried_low, preferred_element_type=jnp.float32
    )
    small_query, small_key = inverse_pull(inverse_grad)
    land_query_grad = (land_query_grad + small_query) / counts[:, None, None]
    land_key_grad = (land_key_grad + small_key) / counts[:, None, None]
    grad_queries = grad_queries + jnp.einsum(
        "ts,shd->thd", member_float, land_query_grad, precision=EXACT_PRECISION
    )
    grad_keys = grad_keys + jnp.einsum(
        "ts,shd->thd", member_float, land_key_grad, precision=EXACT_PRECISION
    )
    heads_float = heads_grad.astype(jnp.float32)
    padded_heads = jnp.pad(heads_float, ((half_width, half_width), (0, 0), (0, 0)))
    conv_back = jnp.zeros(heads_float.shape, jnp.float32)
    conv_terms = []
    for offset in range(KW):
        weighted = heads_float * valid_list[offset][:, None, None]
        conv_terms.append(jnp.sum(weighted * padded_values[offset : offset + row_len], axis=(0, 2)))
        start = 2 * half_width - offset
        shifted_valid = jnp.pad(valid_list[offset], (half_width, half_width))[
            start : start + row_len
        ]
        shifted_weighted = padded_heads[start : start + row_len] * shifted_valid[:, None, None]
        conv_back = conv_back + shifted_weighted * conv_float[:, offset][None, :, None]
    grad_conv = jnp.stack(conv_terms, axis=1)
    grad_values = grad_values + conv_back
    query_low = grad_queries.astype(jnp.bfloat16).reshape(row_len, local_heads * HEAD_DIM)
    key_low = grad_keys.astype(jnp.bfloat16).reshape(row_len, local_heads * HEAD_DIM)
    value_low = grad_values.astype(jnp.bfloat16).reshape(row_len, local_heads * HEAD_DIM)
    grad_query = qk_scale * jnp.einsum(
        "tc,tk->ck", all_tokens, query_low, preferred_element_type=jnp.float32
    )
    grad_key = qk_scale * jnp.einsum(
        "tc,tk->ck", all_tokens, key_low, preferred_element_type=jnp.float32
    )
    grad_value = jnp.einsum("tc,tk->ck", all_tokens, value_low, preferred_element_type=jnp.float32)
    scaled_part = jnp.einsum("tc,dc->td", query_low, w_query, preferred_element_type=jnp.float32)
    scaled_part = scaled_part + jnp.einsum(
        "tc,dc->td", key_low, w_key, preferred_element_type=jnp.float32
    )
    attn_input = lax.psum_scatter(
        (
            qk_scale * scaled_part
            + jnp.einsum("tc,dc->td", value_low, w_value, preferred_element_type=jnp.float32)
        ).astype(jnp.bfloat16),
        "head",
        scatter_dimension=0,
        tiled=True,
    ).astype(jnp.float32)
    input_grad = (first_in_grad + attn_input).astype(jnp.bfloat16)
    summed = lax.psum(
        (grad_query, grad_key, grad_value, grad_output, grad_conv, grad_inner, grad_outer), "batch"
    )
    norm_totals = lax.psum(
        (grad_first_gain, grad_first_bias, grad_second_gain, grad_second_bias), ("batch", "head")
    )
    return (
        layer_out,
        input_grad,
        summed[0],
        summed[1],
        summed[2],
        summed[3],
        summed[4],
        norm_totals[0],
        norm_totals[1],
        summed[5],
        summed[6],
        norm_totals[2],
        norm_totals[3],
    )


def solution(mesh):
    placed = (
        P(("batch", "head"), None),
        P("batch"),
        P("batch"),
        P("batch"),
        P(None, "head"),
        P(None, "head"),
        P(None, "head"),
        P("head", None),
        P("head", None),
        P(),
        P(),
        P(),
        P(),
        P(),
        P(),
        P(("batch", "head"), None),
    )
    return jax.shard_map(
        shards,
        mesh=mesh,
        in_specs=placed,
        out_specs=(
            P(("batch", "head"), None),
            P(("batch", "head"), None),
            P(None, "head"),
            P(None, "head"),
            P(None, "head"),
            P("head", None),
            P("head", None),
            P(),
            P(),
            P(None, "head"),
            P("head", None),
            P(),
            P(),
        ),
        check_vma=False,
    )
```

profile of v0, /device:TPU:0, one launch (start us, length us, event | category | flops | bytes accessed | tf_op | source)
XLA Modules:
  0.0 913.9 jit_solution(11133062830195507953)
XLA Ops:
  24.1 34.7 %all-gather.3.cloned.1.call-done = bf16[4096,768]{1,0:T(8,128)(2,1)} async-done(((bf16[1024,768]{1,0:T(8,128)(2,1)}), bf16[4096,768]{1,0:T(8,128)(2,1)}) %all-gather.3.cloned.1.call-update) | async-done | bytes 6291472 | tf_op jit(solution)/shard_map/all_gather | solution.py:72
  85.9 12.5 %convolution_multiply_fusion.6 = f32[3,4,64,64]{3,2,1,0:T(8,128)S(1)} fusion(f32[3,4,64,64]{3,2,1,0:T(8,128)S(1)} %convolution_multiply_fusion.7, f32[3,4,64,64]{3,2,1,0:T(8,128)S(1)} %convolution_subtract_fusion.2), kind=kOutput, calls=%fused_computation.274 | convolution fusion | flops 37797888 | bytes 589824 | tf_op jit(solution)/shard_map/jvp()/dot_general | solution.py:25
  101.8 6.7 select_reduce_fusion.1
  108.5 8.1 exponential_reduce_fusion.1
  130.2 7.4 select_reduce_fusion
  137.7 7.2 exponential_reduce_fusion
  145.5 34.2 %fusion.14 = bf16[4096,3,64]{0,2,1:T(8,128)(2,1)} fusion(bf16[3,256,64]{2,1,0:T(8,128)(2,1)S(1)} %bitcast.347, f32[4096]{0:T(1024)} %get-tuple-element.146, f32[3]{0:T(128)} %get-tuple-element.67, f32[4096]{0:T(1024)} %get-tuple-element.145, f32[3]{0:T(128)} %get-tuple-element.68, f32[4096]{0:T(1024)} %get-tuple-element.144, f32[3]{0:T(128)} %get-tuple-element.69, ...), kind=kOutput, calls=%fused_computation.78 | convolution fusion | flops 492306432 | bytes 20611468 | tf_op jit(solution)/shard_map/hts,hsd->thd/dot_general | solution.py:137
  179.8 6.0 convolution_convert_fusion
  185.9 58.4 %reduce-scatter.5.cloned.1.call-done = bf16[1024,768]{1,0:T(8,128)(2,1)} async-done(((bf16[4096,768]{1,0:T(8,128)(2,1)}), bf16[1024,768]{1,0:T(8,128)(2,1)}) %reduce-scatter.5.cloned.1.call-update) | async-done | bytes 1572880 | tf_op jit(solution)/shard_map/reduce_scatter | solution.py:157
  247.2 37.5 %multiply_convert_fusion.2 = (bf16[1024,3072]{1,0:T(8,128)(2,1)S(1)}, f32[1024,3072]{1,0:T(8,128)}, f32[1024,3072]{1,0:T(8,128)}) fusion(bf16[768,3072]{1,0:T(8,128)(2,1)} %param.27, f32[768]{0:T(1024)S(1)} %copy-done.141, f32[768]{0:T(1024)S(1)} %copy-done.122, f32[1024]{0:T(1024)S(1)} %add_rsqrt_fusion.1, f32[1024]{0:T(1024)S(1)} %broadcast_multiply_fusion.5, ...), kind=kOutput, calls=%fused_computation.42 | convolution fusion | flops 5042601984 | bytes 39335936 | tf_op jit(solution)/shard_map/dot_general | solution.py:167
  296.2 17.6 %add_convert_fusion.1 = bf16[1024,3072]{1,0:T(8,128)(2,1)} fusion(f32[1024,3072]{1,0:T(8,128)} %get-tuple-element.111, f32[1024,3072]{1,0:T(8,128)} %get-tuple-element.155, bf16[3072,768]{1,0:T(8,128)(2,1)} %param.28, bf16[1024,768]{1,0:T(8,128)(2,1)} %param.31, f32[1024,768]{1,0:T(8,128)} %copy-done.26, f32[1024]{0:T(1024)S(1)} %broadcast_multiply_fusion.2, ...), kind=kOutput, calls=%fused_computation.41 | convolution fusion | flops 4882956288 | bytes 40913920 | tf_op jit(solution)/shard_map/td,fd->tf/dot_general | solution.py:179
  313.7 12.2 %multiply_reduce_fusion.2 = (f32[768]{0:T(1024)}, f32[1024]{0:T(1024)S(1)}, f32[1024]{0:T(1024)S(1)}, f32[768]{0:T(1024)}, f32[1024,768]{1,0:T(8,128)S(1)}) fusion(f32[1024]{0:T(1024)S(1)} %add_rsqrt_fusion.1, f32[1024]{0:T(1024)S(1)} %broadcast_multiply_fusion.5, bf16[1024,768]{1,0:T(8,128)(2,1)S(1)} %copy-done.10, bf16[1024,768]{1,0:T(8,128)(2,1)S(1)} %copy-done.6, ...), kind=kOutput, calls=%fused_computation.186 | convolution fusion | flops 4848349184 | bytes 22065152 | tf_op jit(solution)/shard_map/tf,df->td/dot_general | solution.py:181
  329.9 12.1 %convolution_convert_fusion.1 = bf16[3072,768]{1,0:T(8,128)(2,1)} fusion(bf16[1024,3072]{1,0:T(8,128)(2,1)} %copy-done.142, bf16[1024,768]{1,0:T(8,128)(2,1)} %param.31, f32[1024,768]{1,0:T(8,128)} %copy-done.26, f32[1024]{0:T(1024)S(1)} %broadcast_multiply_fusion.2, f32[1024]{0:T(1024)S(1)} %broadcast_multiply_fusion.3, f32[768]{0:T(1024)S(1)} %copy-done.136, ...), kind=kOutput, calls=%fused_computation.76 | convolution fusion | flops 4841275392 | bytes 15748096 | tf_op jit(solution)/shard_map/tf,td->fd/dot_general | solution.py:188
  366.0 10.2 %convolution_convert_fusion.2 = bf16[768,3072]{1,0:T(8,128)(2,1)} fusion(bf16[1024,3072]{1,0:T(8,128)(2,1)} %add_convert_fusion.1, f32[768]{0:T(1024)S(1)} %copy-done.141, f32[768]{0:T(1024)S(1)} %copy-done.122, bf16[1024,768]{1,0:T(8,128)(2,1)S(1)} %copy-done.10, bf16[1024,768]{1,0:T(8,128)(2,1)S(1)} %copy-done.6, f32[1024]{0:T(1024)S(1)} %add_rsqrt_fusion.1, ...), kind=kOutput, calls=%fused_computation.77 | convolution fusion | flops 4840488960 | bytes 14170112 | tf_op jit(solution)/shard_map/td,tf->df/dot_general | solution.py:187
  377.0 6.1 multiply_reduce_fusion.3
  383.1 9.0 fusion.175
  426.8 8.7 multiply_reduce_fusion.1
  445.6 10.8 %multiply_reduce_fusion = (f32[3,256]{1,0:T(4,128)S(1)}, f32[3,256,4096]{2,1,0:T(8,128)}) fusion(f32[3,256,4096]{2,1,0:T(8,128)} %get-tuple-element.152, f32[3,256]{1,0:T(4,128)S(1)} %copy-done.111, pred[256,4096]{1,0:T(8,128)(4,1)S(1)} %copy-done.5, bf16[3,256,64]{2,1,0:T(8,128)(2,1)S(1)} %bitcast.343, bf16[4096,3,64]{0,2,1:T(8,128)(2,1)} %bitcast.328), kind=kOutput, calls=%fused_computation.38 | convolution fusion | flops 415235328 | bytes 27891712 | tf_op jit(solution)/shard_map/hsd,thd->hst/dot_general | solution.py:223
  458.2 10.2 %multiply_convert_fusion.1 = bf16[3,4096,256]{1,2,0:T(8,128)(2,1)S(1)} fusion(f32[3,4096,256]{1,2,0:T(8,128)} %get-tuple-element.166, f32[3,4096,256]{1,2,0:T(8,128)} %get-tuple-element.154, f32[3,4096]{1,0:T(4,128)S(1)} %copy-done.109, f32[3,4096]{1,0:T(4,128)S(1)} %copy-done.95, pred[4096,256]{0,1:T(8,128)(4,1)} %broadcast_compare_fusion), kind=kLoop, calls=%fused_computation.39 | loop fusion | flops 15728640 | bytes 32604160 | tf_op jit(solution)/shard_map/convert_element_type | solution.py:209
  470.5 7.5 multiply_convert_fusion
  480.1 5.9 fusion.24
  488.1 5.9 fusion.26
  496.7 6.5 fusion.295
  503.1 6.3 fusion.294
  511.4 58.6 %fusion.17 = bf16[4096,3,64]{0,2,1:T(8,128)(2,1)S(1)} fusion(bf16[3,256,64]{2,1,0:T(8,128)(2,1)S(1)} %bitcast.344, f32[4096,3,64]{0,2,1:T(8,128)} %fusion.270, f32[4096]{0:T(1024)} %get-tuple-element.171, f32[4096]{0:T(1024)} %get-tuple-element.172, f32[4096]{0:T(1024)} %get-tuple-element.173, f32[4096]{0:T(1024)} %get-tuple-element.174, ...), kind=kOutput, calls=%fused_computation.81 | convolution fusion | flops 492306432 | bytes 20569484 | tf_op jit(solution)/shard_map/hst,hsd->thd/dot_general | solution.py:233
  571.2 12.4 %add_convert_fusion = bf16[4096,768]{1,0:T(8,128)(2,1)} fusion(f32[4096,768]{1,0:T(8,128)} %fusion.294, f32[4096,768]{1,0:T(8,128)} %fusion.295, bf16[4096,192]{0,1:T(8,128)(2,1)S(1)} %bitcast.337, bf16[768,192]{0,1:T(8,128)(2,1)S(1)} %copy-done.104), kind=kOutput, calls=%fused_computation.36 | convolution fusion | flops 1220542464 | bytes 33325056 | tf_op jit(solution)/shard_map/tc,dc->td/dot_general | solution.py:277
  584.3 40.5 %all-reduce.36 = (f32[768]{0:T(1024)}, f32[768]{0:T(1024)}, f32[768]{0:T(1024)}, f32[768]{0:T(1024)}) all-reduce(f32[768]{0:T(1024)S(1)} %copy-done.137, f32[768]{0:T(1024)S(1)} %copy-done.138, f32[768]{0:T(1024)S(1)} %copy-done.124, f32[768]{0:T(1024)S(1)} %copy-done.125), channel_id=1, replica_groups=mesh['batch'=8,'head'=4] {'batch','head'}, use_global_device_ids=true, to_apply=%region_62.63 | all-reduce | flops 3072 | bytes 24576 | tf_op jit(solution)/shard_map/psum | solution.py:287
  624.9 8.3 fusion.117
  633.8 8.3 fusion.115
  658.2 8.3 fusion.113
  668.6 9.2 %fusion.111 = (f32[3]{0:T(128)}, f32[3]{0:T(128)}, f32[3]{0:T(128)}, f32[3]{0:T(128)}, f32[3]{0:T(128)}, /*index=5*/f32[3]{0:T(128)}, f32[3]{0:T(128)}, f32[3]{0:T(128)}) fusion(f32[4096]{0:T(1024)} %get-tuple-element.143, f32[4096,3,64]{0,2,1:T(8,128)S(1)} %copy-done.2, bf16[4096,3,64]{0,2,1:T(8,128)(2,1)} %bitcast.320, pred[4096]{0:T(1024)(128)(4,1)S(1)} %copy-done.91, ...), kind=kLoop, calls=%fused_computation.179 | loop fusion | flops 20447208 | bytes 4853856 | tf_op jit(solution)/shard_map/reduce_sum | solution.py:251
  685.5 209.9 %all-reduce.43 = (f32[3,33]{1,0:T(4,128)}, f32[768,768]{1,0:T(8,128)}, f32[768,768]{1,0:T(8,128)}) all-reduce(f32[3,33]{1,0:T(4,128)S(1)} %stack.135, bf16[768,768]{1,0:T(8,128)(2,1)} %reduce-scatter.9.cloned.1.call-done, bf16[768,768]{1,0:T(8,128)(2,1)} %reduce-scatter.11.cloned.1.call-done), channel_id=1, replica_groups=mesh['batch'=8,'head'=4] {'batch'}, use_global_device_ids=true, to_apply=%region_60.61 | all-reduce | flops 1179747 | bytes 7078680 | tf_op jit(solution)/shard_map/psum | solution.py:284
  (535 shorter events, 199.4 us)
Async XLA Ops:
  7.2 172.6 %copy-start = (bf16[192,768]{1,0:T(8,128)(2,1)S(1)}, bf16[192,768]{1,0:T(8,128)(2,1)}, u32[]{:S(2)}) copy-start(bf16[192,768]{1,0:T(8,128)(2,1)} %param.23) | copy-start | bytes 884740
  7.2 51.5 %copy-start.107 = (bf16[768,192]{0,1:T(8,128)(2,1)S(1)}, bf16[768,192]{0,1:T(8,128)(2,1)}, u32[]{:S(2)}) copy-start(bf16[768,192]{0,1:T(8,128)(2,1)} %param.20) | copy-start | bytes 884740
  7.2 51.5 %all-gather.3.cloned.1.call-start = ((), (), s32[]{:S(2)}) async-start(), calls=%async_computation.4 | async-start | bytes 7864320 | tf_op jit(solution)/shard_map/all_gather | solution.py:72
  8.0 236.4 %reduce-scatter.5.cloned.1.call-start = ((), (), s32[]{:S(2)}) async-start(), calls=%async_computation.5 | async-start | bytes 7864320 | tf_op jit(solution)/shard_map/reduce_scatter | solution.py:157
  10.6 88.6 %copy-start.44 = (f32[64,64]{1,0:T(8,128)}, f32[64,64]{1,0:T(8,128)S(1)}, u32[]{:S(2)}) copy-start(f32[64,64]{1,0:T(8,128)S(1)} %get-tuple-element.169) | copy-start | bytes 49156
  11.4 56.1 %copy-start.90 = (pred[4096]{0:T(1024)(128)(4,1)}, pred[4096]{0:T(1024)(128)(4,1)S(1)}, u32[]{:S(2)}) copy-start(pred[4096]{0:T(1024)(128)(4,1)S(1)} %get-tuple-element.113) | copy-start | bytes 12292
  11.4 134.1 %copy-start.99 = (f32[4096]{0:T(1024)}, f32[4096]{0:T(1024)S(1)}, u32[]{:S(2)}) copy-start(f32[4096]{0:T(1024)S(1)} %get-tuple-element.112) | copy-start | bytes 49156
  12.1 55.3 %copy-start.96 = (s32[4096]{0:T(1024)}, s32[4096]{0:T(1024)S(1)}, u32[]{:S(2)}) copy-start(s32[4096]{0:T(1024)S(1)} %multiply_add_fusion.1) | copy-start | bytes 49156
  13.6 55.3 %copy-start.120 = (f32[256]{0:T(256)}, f32[256]{0:T(256)S(1)}, u32[]{:S(2)}) copy-start(f32[256]{0:T(256)S(1)} %convert_reduce_fusion.1) | copy-start | bytes 3076
  24.0 77.7 %copy-start.4 = (pred[256,4096]{1,0:T(8,128)(4,1)}, pred[256,4096]{1,0:T(8,128)(4,1)S(1)}, u32[]{:S(2)}) copy-start(pred[256,4096]{1,0:T(8,128)(4,1)S(1)} %compare_and_fusion) | copy-start | bytes 3145732
  68.9 61.3 %copy-start.75 = (bf16[256,3,64]{0,2,1:T(8,128)(2,1)}, bf16[256,3,64]{0,2,1:T(8,128)(2,1)S(1)}, u32[]{:S(2)}) copy-start(bf16[256,3,64]{0,2,1:T(8,128)(2,1)S(1)} %get-tuple-element.147) | copy-start | bytes 294916
  185.8 58.5 %copy-start.6 = (bf16[1024,768]{1,0:T(8,128)(2,1)S(1)}, bf16[1024,768]{1,0:T(8,128)(2,1)}, u32[]{:S(2)}) copy-start(bf16[1024,768]{1,0:T(8,128)(2,1)} %param.16) | copy-start | bytes 4718596
  185.8 61.3 %copy-start.122 = (f32[768]{0:T(1024)S(1)}, f32[768]{0:T(1024)}, u32[]{:S(2)}) copy-start(f32[768]{0:T(1024)} %param.25) | copy-start | bytes 9220
  185.8 61.3 %copy-start.141 = (f32[768]{0:T(1024)S(1)}, f32[768]{0:T(1024)}, u32[]{:S(2)}) copy-start(f32[768]{0:T(1024)} %param.26) | copy-start | bytes 9220
  185.8 190.7 %all-gather.5.cloned.1.call-start = ((), (), s32[]{:S(2)}) async-start(), calls=%async_computation.6 | async-start | bytes 7864320 | tf_op jit(solution)/shard_map/all_gather | solution.py:197
  244.3 40.4 %slice-start.13 = ((s8[4718592]{0:T(1024)(128)(4,1)}), s8[4194304]{0:T(1024)(128)(4,1)S(1)}, s32[]{:S(2)}) async-start(s8[4718592]{0:T(1024)(128)(4,1)} %bitcast.394), calls=%async_computation.24 | async-start | bytes 8388608
  246.4 119.6 %copy-start.112 = (f32[1024]{0:T(1024)}, f32[1024]{0:T(1024)S(1)}, u32[]{:S(2)}) copy-start(f32[1024]{0:T(1024)S(1)} %broadcast_multiply_fusion.5) | copy-start | bytes 12292
  247.2 118.8 %copy-start.114 = (f32[1024]{0:T(1024)}, f32[1024]{0:T(1024)S(1)}, u32[]{:S(2)}) copy-start(f32[1024]{0:T(1024)S(1)} %add_rsqrt_fusion.1) | copy-start | bytes 12292
  247.2 37.5 %slice-start.14 = ((s8[4718592]{0:T(1024)(128)(4,1)}), s8[524288]{0:T(1024)(128)(4,1)S(1)}, s32[]{:S(2)}) async-start(s8[4718592]{0:T(1024)(128)(4,1)} %bitcast.394), calls=%async_computation.25 | async-start | bytes 1048576
  329.8 355.7 %reduce-scatter.11.cloned.1.call-start = ((), (), s32[]{:S(2)}) async-start(), calls=%async_computation.9 | async-start | bytes 5898240 | tf_op jit(solution)/shard_map/reduce_scatter | solution.py:193
  342.0 343.5 %reduce-scatter.9.cloned.1.call-start = ((), (), s32[]{:S(2)}) async-start(), calls=%async_computation.8 | async-start | bytes 5898240 | tf_op jit(solution)/shard_map/reduce_scatter | solution.py:190
  376.3 519.1 %reduce-scatter.7.cloned.1.call-start = ((), (), s32[]{:S(2)}) async-start(), calls=%async_computation.7 | async-start | bytes 7864320 | tf_op jit(solution)/shard_map/reduce_scatter | solution.py:274
  383.1 128.3 %copy-start.3 = (bf16[4096,192]{0,1:T(8,128)(2,1)}, bf16[4096,192]{0,1:T(8,128)(2,1)S(1)}, u32[]{:S(2)}) copy-start(bf16[4096,192]{0,1:T(8,128)(2,1)S(1)} %get-tuple-element.168) | copy-start | bytes 4718596
  511.4 59.8 %copy-start.104 = (bf16[768,192]{0,1:T(8,128)(2,1)S(1)}, bf16[768,192]{0,1:T(8,128)(2,1)}, u32[]{:S(2)}) copy-start(bf16[768,192]{0,1:T(8,128)(2,1)} %param.22) | copy-start | bytes 884740
  583.6 41.2 %copy-start.2 = (f32[4096,3,64]{0,2,1:T(8,128)S(1)}, f32[4096,3,64]{0,2,1:T(8,128)}, u32[]{:S(2)}) copy-start(f32[4096,3,64]{0,2,1:T(8,128)} %convert_element_type.180) | copy-start | bytes 9437188
  583.7 316.3 %all-reduce.42.cloned.1.call-start = ((), (), s32[]{:S(2)}) async-start(), calls=%async_computation.10 | async-start | bytes 4718592 | tf_op jit(solution)/shard_map/psum | solution.py:284
  668.6 226.8 %copy-start.113 = (f32[1024]{0:T(1024)S(1)}, f32[1024]{0:T(1024)}, u32[]{:S(2)}) copy-start(f32[1024]{0:T(1024)} %copy-done.112) | copy-start | bytes 12292
  668.6 226.8 %copy-start.115 = (f32[1024]{0:T(1024)S(1)}, f32[1024]{0:T(1024)}, u32[]{:S(2)}) copy-start(f32[1024]{0:T(1024)} %copy-done.114) | copy-start | bytes 12292
  668.6 226.8 %copy-start.117 = (f32[1024]{0:T(1024)S(1)}, f32[1024]{0:T(1024)}, u32[]{:S(2)}) copy-start(f32[1024]{0:T(1024)} %copy-done.116) | copy-start | bytes 12292
  668.6 226.8 %copy-start.119 = (f32[1024]{0:T(1024)S(1)}, f32[1024]{0:T(1024)}, u32[]{:S(2)}) copy-start(f32[1024]{0:T(1024)} %copy-done.118) | copy-start | bytes 12292
  668.6 226.9 %copy-start.123 = (f32[768]{0:T(1024)S(1)}, f32[768]{0:T(1024)}, u32[]{:S(2)}) copy-start(f32[768]{0:T(1024)} %param.25) | copy-start | bytes 9220
  677.8 217.6 %copy-start.7 = (bf16[1024,768]{1,0:T(8,128)(2,1)S(1)}, bf16[1024,768]{1,0:T(8,128)(2,1)}, u32[]{:S(2)}) copy-start(bf16[1024,768]{1,0:T(8,128)(2,1)} %param.16) | copy-start | bytes 4718596
  (133 other events, 876.7 us)
Sparse Core Ops, SparseCore 0:
  9.6 49.0 all-gather.2
  185.9 58.3 reduce-scatter.4
  330.0 46.4 all-gather.4
  379.0 47.8 reduce-scatter.10
  429.3 47.8 reduce-scatter.8
  583.8 59.5 reduce-scatter.6
  658.3 148.6 all-reduce.41
where the time goes:
time: 925 us; the launch traced here: 914 us
  matrix products  393 us (42%)
  blocking collectives  250 us (27%)
  other arithmetic  101 us (11%)
  waiting for transfers between devices  94.1 us (10%)
  local copies, waits for them, and re-layouts  57.7 us (6%)
  between operations  17.2 us (2%)
    psum x1, blocking collectives, shards(): lax.psum((grad_query, grad_key, grad_value, grad_output, grad_conv, grad_...  210 us
    dot_general x1, matrix products, shards(): jnp.einsum('hst,hsd->thd', third_low, carried_low, preferred_element_type...  58.6 us
    reduce_scatter x1, waiting for transfers between devices, shards(): lax.psum_scatter(jnp.dot(heads_out, w_output, preferred_element_type=jnp....  58.4 us
    psum x1, blocking collectives, shards(): lax.psum((grad_first_gain, grad_first_bias, grad_second_gain, grad_second...  40.5 us
    dot_general x1, matrix products, shards(): inner_pre = jnp.dot(norm_low, w_inner, preferred_element_type=jnp.float32)  37.5 us
    all_gather x1, waiting for transfers between devices, shards(): all_tokens = lax.all_gather(tokens_in, 'head', axis=0, tiled=True)  34.7 us
    reduce_sum x5, other arithmetic, shards(): jnp.sum(weighted * padded_values[offset:offset + row_len], axis=(0, 2))  34.2 us
    dot_general x1, matrix products, shards(): jnp.einsum('hts,hsd->thd', first_low, mixed_low, preferred_element_type=j...  34.2 us
  transfers between devices with their start and end apart: 7, of which 3 were waited for; matrix products, arithmetic and copies ran while one was open for 36% of the time, Pallas kernels for 0%

commit v1 on v0

--- a/solution.py
+++ b/solution.py
@@ -284,9 +284,9 @@
     summed = lax.psum(
         (grad_query, grad_key, grad_value, grad_output, grad_conv, grad_inner, grad_outer), "batch"
     )
-    norm_totals = lax.psum(
-        (grad_first_gain, grad_first_bias, grad_second_gain, grad_second_bias), ("batch", "head")
-    )
+    norm_totals = (grad_first_gain, grad_first_bias, grad_second_gain, grad_second_bias)
+    for mesh_axis in ("head", "batch"):
+        norm_totals = lax.psum(norm_totals, mesh_axis)
     return (
         layer_out,
         input_grad,

time: 925 us -> 895 us (0.968)
  blocking collectives: 250 us -> 220 us
    psum x1, blocking collectives: 40.5 us -> 11.1 us  [shards(): norm_totals = lax.psum(norm_totals, mesh_axis)]
  transfers between devices with their start and end apart: 7 -> 7, of which waited for: 3 -> 3; matrix products, arithmetic and copies ran while one was open for 36% -> 37% of each run, Pallas kernels for 0% -> 0%
where the time goes in v1:
time: 895 us; the launch traced here: 884 us
  matrix products  393 us (44%)
  blocking collectives  220 us (25%)
  other arithmetic  101 us (11%)
  waiting for transfers between devices  94.1 us (11%)
  local copies, waits for them, and re-layouts  57.7 us (6%)
  between operations  17.2 us (2%)
    psum x1, blocking collectives, shards(): lax.psum((grad_query, grad_key, grad_value, grad_output, grad_conv, grad_...  209 us
    dot_general x1, matrix products, shards(): jnp.einsum('hst,hsd->thd', third_low, carried_low, preferred_element_type...  58.6 us
    reduce_scatter x1, waiting for transfers between devices, shards(): lax.psum_scatter(jnp.dot(heads_out, w_output, preferred_element_type=jnp....  58.4 us
    dot_general x1, matrix products, shards(): inner_pre = jnp.dot(norm_low, w_inner, preferred_element_type=jnp.float32)  37.5 us
    all_gather x1, waiting for transfers between devices, shards(): all_tokens = lax.all_gather(tokens_in, 'head', axis=0, tiled=True)  34.7 us
    reduce_sum x5, other arithmetic, shards(): jnp.sum(weighted * padded_values[offset:offset + row_len], axis=(0, 2))  34.4 us
    dot_general x1, matrix products, shards(): jnp.einsum('hts,hsd->thd', first_low, mixed_low, preferred_element_type=j...  34.2 us
    dot_general x18, matrix products, newton_inverse(): jnp.matmul(estimate, factor_term, precision=EXACT_PRECISION)  26.2 us
  transfers between devices with their start and end apart: 7, of which 3 were waited for; matrix products, arithmetic and copies ran while one was open for 37% of the time, Pallas kernels for 0%

profile of v1, /device:TPU:0, one launch (start us, length us, event | category | flops | bytes accessed | tf_op | source)
XLA Modules:
  0.0 884.0 jit_solution(6286977714259474386)
XLA Ops:
  24.1 34.7 %all-gather.3.cloned.1.call-done = bf16[4096,768]{1,0:T(8,128)(2,1)} async-done(((bf16[1024,768]{1,0:T(8,128)(2,1)}), bf16[4096,768]{1,0:T(8,128)(2,1)}) %all-gather.3.cloned.1.call-update) | async-done | bytes 6291472 | tf_op jit(solution)/shard_map/all_gather | solution.py:72
  85.9 12.5 %convolution_multiply_fusion.6 = f32[3,4,64,64]{3,2,1,0:T(8,128)S(1)} fusion(f32[3,4,64,64]{3,2,1,0:T(8,128)S(1)} %convolution_multiply_fusion.7, f32[3,4,64,64]{3,2,1,0:T(8,128)S(1)} %convolution_subtract_fusion.2), kind=kOutput, calls=%fused_computation.274 | convolution fusion | flops 37797888 | bytes 589824 | tf_op jit(solution)/shard_map/jvp()/dot_general | solution.py:25
  101.8 6.7 select_reduce_fusion.1
  108.5 8.1 exponential_reduce_fusion.1
  130.2 7.4 select_reduce_fusion
  137.7 7.2 exponential_reduce_fusion
  145.5 34.2 %fusion.14 = bf16[4096,3,64]{0,2,1:T(8,128)(2,1)} fusion(bf16[3,256,64]{2,1,0:T(8,128)(2,1)S(1)} %bitcast.347, f32[4096]{0:T(1024)} %get-tuple-element.150, f32[3]{0:T(128)} %get-tuple-element.67, f32[4096]{0:T(1024)} %get-tuple-element.149, f32[3]{0:T(128)} %get-tuple-element.68, f32[4096]{0:T(1024)} %get-tuple-element.148, f32[3]{0:T(128)} %get-tuple-element.69, ...), kind=kOutput, calls=%fused_computation.78 | convolution fusion | flops 492306432 | bytes 20611468 | tf_op jit(solution)/shard_map/hts,hsd->thd/dot_general | solution.py:137
  179.8 6.0 convolution_convert_fusion
  185.9 58.4 %reduce-scatter.5.cloned.1.call-done = bf16[1024,768]{1,0:T(8,128)(2,1)} async-done(((bf16[4096,768]{1,0:T(8,128)(2,1)}), bf16[1024,768]{1,0:T(8,128)(2,1)}) %reduce-scatter.5.cloned.1.call-update) | async-done | bytes 1572880 | tf_op jit(solution)/shard_map/reduce_scatter | solution.py:157
  247.2 37.5 %multiply_convert_fusion.2 = (bf16[1024,3072]{1,0:T(8,128)(2,1)S(1)}, f32[1024,3072]{1,0:T(8,128)}, f32[1024,3072]{1,0:T(8,128)}) fusion(bf16[768,3072]{1,0:T(8,128)(2,1)} %param.27, f32[768]{0:T(1024)S(1)} %copy-done.141, f32[768]{0:T(1024)S(1)} %copy-done.122, f32[1024]{0:T(1024)S(1)} %add_rsqrt_fusion.1, f32[1024]{0:T(1024)S(1)} %broadcast_multiply_fusion.5, ...), kind=kOutput, calls=%fused_computation.42 | convolution fusion | flops 5042601984 | bytes 39335936 | tf_op jit(solution)/shard_map/dot_general | solution.py:167
  296.2 17.6 %add_convert_fusion.1 = bf16[1024,3072]{1,0:T(8,128)(2,1)} fusion(f32[1024,3072]{1,0:T(8,128)} %get-tuple-element.115, f32[1024,3072]{1,0:T(8,128)} %get-tuple-element.159, bf16[3072,768]{1,0:T(8,128)(2,1)} %param.28, bf16[1024,768]{1,0:T(8,128)(2,1)} %param.31, f32[1024,768]{1,0:T(8,128)} %copy-done.26, f32[1024]{0:T(1024)S(1)} %broadcast_multiply_fusion.2, ...), kind=kOutput, calls=%fused_computation.41 | convolution fusion | flops 4882956288 | bytes 40913920 | tf_op jit(solution)/shard_map/td,fd->tf/dot_general | solution.py:179
  313.7 12.2 %multiply_reduce_fusion.2 = (f32[768]{0:T(1024)}, f32[1024]{0:T(1024)S(1)}, f32[1024]{0:T(1024)S(1)}, f32[768]{0:T(1024)}, f32[1024,768]{1,0:T(8,128)S(1)}) fusion(f32[1024]{0:T(1024)S(1)} %add_rsqrt_fusion.1, f32[1024]{0:T(1024)S(1)} %broadcast_multiply_fusion.5, bf16[1024,768]{1,0:T(8,128)(2,1)S(1)} %copy-done.10, bf16[1024,768]{1,0:T(8,128)(2,1)S(1)} %copy-done.6, ...), kind=kOutput, calls=%fused_computation.186 | convolution fusion | flops 4848349184 | bytes 22065152 | tf_op jit(solution)/shard_map/tf,df->td/dot_general | solution.py:181
  329.9 12.1 %convolution_convert_fusion.1 = bf16[3072,768]{1,0:T(8,128)(2,1)} fusion(bf16[1024,3072]{1,0:T(8,128)(2,1)} %copy-done.142, bf16[1024,768]{1,0:T(8,128)(2,1)} %param.31, f32[1024,768]{1,0:T(8,128)} %copy-done.26, f32[1024]{0:T(1024)S(1)} %broadcast_multiply_fusion.2, f32[1024]{0:T(1024)S(1)} %broadcast_multiply_fusion.3, f32[768]{0:T(1024)S(1)} %copy-done.136, ...), kind=kOutput, calls=%fused_computation.76 | convolution fusion | flops 4841275392 | bytes 15748096 | tf_op jit(solution)/shard_map/tf,td->fd/dot_general | solution.py:188
  366.0 10.2 %convolution_convert_fusion.2 = bf16[768,3072]{1,0:T(8,128)(2,1)} fusion(bf16[1024,3072]{1,0:T(8,128)(2,1)} %add_convert_fusion.1, f32[768]{0:T(1024)S(1)} %copy-done.141, f32[768]{0:T(1024)S(1)} %copy-done.122, bf16[1024,768]{1,0:T(8,128)(2,1)S(1)} %copy-done.10, bf16[1024,768]{1,0:T(8,128)(2,1)S(1)} %copy-done.6, f32[1024]{0:T(1024)S(1)} %add_rsqrt_fusion.1, ...), kind=kOutput, calls=%fused_computation.77 | convolution fusion | flops 4840488960 | bytes 14170112 | tf_op jit(solution)/shard_map/td,tf->df/dot_general | solution.py:187
  377.0 6.1 multiply_reduce_fusion.3
  383.1 9.0 %fusion.175 = f32[3,256,64]{2,1,0:T(8,128)S(1)} fusion(f32[3,4096,256]{1,2,0:T(8,128)} %get-tuple-element.158, f32[3,4096]{1,0:T(4,128)S(1)} %copy-done.93, pred[4096,256]{0,1:T(8,128)(4,1)S(1)} %copy-done.9, bf16[4096,3,64]{0,2,1:T(8,128)(2,1)S(1)} %bitcast.313, pred[4096]{0:T(1024)(128)(4,1)S(1)} %copy-done.91), kind=kOutput, calls=%fused_computation.320 | convolution fusion | flops 412876800 | bytes 15454208 | tf_op jit(solution)/shard_map/reshape | solution.py:216
  426.8 8.7 multiply_reduce_fusion.1
  445.6 10.8 %multiply_reduce_fusion = (f32[3,256]{1,0:T(4,128)S(1)}, f32[3,256,4096]{2,1,0:T(8,128)}) fusion(f32[3,256,4096]{2,1,0:T(8,128)} %get-tuple-element.156, f32[3,256]{1,0:T(4,128)S(1)} %copy-done.111, pred[256,4096]{1,0:T(8,128)(4,1)S(1)} %copy-done.5, bf16[3,256,64]{2,1,0:T(8,128)(2,1)S(1)} %bitcast.343, bf16[4096,3,64]{0,2,1:T(8,128)(2,1)} %bitcast.328), kind=kOutput, calls=%fused_computation.38 | convolution fusion | flops 415235328 | bytes 27891712 | tf_op jit(solution)/shard_map/hsd,thd->hst/dot_general | solution.py:223
  458.2 10.2 %multiply_convert_fusion.1 = bf16[3,4096,256]{1,2,0:T(8,128)(2,1)S(1)} fusion(f32[3,4096,256]{1,2,0:T(8,128)} %get-tuple-element.170, f32[3,4096,256]{1,2,0:T(8,128)} %get-tuple-element.158, f32[3,4096]{1,0:T(4,128)S(1)} %copy-done.109, f32[3,4096]{1,0:T(4,128)S(1)} %copy-done.95, pred[4096,256]{0,1:T(8,128)(4,1)} %broadcast_compare_fusion), kind=kLoop, calls=%fused_computation.39 | loop fusion | flops 15728640 | bytes 32604160 | tf_op jit(solution)/shard_map/convert_element_type | solution.py:209
  470.5 7.5 multiply_convert_fusion
  480.1 5.9 fusion.24
  488.1 5.9 fusion.26
  496.7 6.5 fusion.295
  503.1 6.3 fusion.294
  511.4 58.6 %fusion.17 = bf16[4096,3,64]{0,2,1:T(8,128)(2,1)S(1)} fusion(bf16[3,256,64]{2,1,0:T(8,128)(2,1)S(1)} %bitcast.344, f32[4096,3,64]{0,2,1:T(8,128)} %fusion.270, f32[4096]{0:T(1024)} %get-tuple-element.175, f32[4096]{0:T(1024)} %get-tuple-element.176, f32[4096]{0:T(1024)} %get-tuple-element.177, f32[4096]{0:T(1024)} %get-tuple-element.178, ...), kind=kOutput, calls=%fused_computation.81 | convolution fusion | flops 492306432 | bytes 20569484 | tf_op jit(solution)/shard_map/hst,hsd->thd/dot_general | solution.py:233
  571.2 12.4 %add_convert_fusion = bf16[4096,768]{1,0:T(8,128)(2,1)} fusion(f32[4096,768]{1,0:T(8,128)} %fusion.294, f32[4096,768]{1,0:T(8,128)} %fusion.295, bf16[4096,192]{0,1:T(8,128)(2,1)S(1)} %bitcast.337, bf16[768,192]{0,1:T(8,128)(2,1)S(1)} %copy-done.104), kind=kOutput, calls=%fused_computation.36 | convolution fusion | flops 1220542464 | bytes 33325056 | tf_op jit(solution)/shard_map/tc,dc->td/dot_general | solution.py:277
  584.3 11.1 %all-reduce.38 = (f32[768]{0:T(1024)}, f32[768]{0:T(1024)}, f32[768]{0:T(1024)}, f32[768]{0:T(1024)}) all-reduce(f32[768]{0:T(1024)S(1)} %copy-done.137, f32[768]{0:T(1024)S(1)} %copy-done.138, f32[768]{0:T(1024)S(1)} %copy-done.124, f32[768]{0:T(1024)S(1)} %copy-done.125), channel_id=1, replica_groups=mesh['batch'=8,'head'=4] {'head'}, use_global_device_ids=true, to_apply=%region_62.63 | all-reduce | flops 3072 | bytes 24576 | tf_op jit(solution)/shard_map/psum | solution.py:289
  595.4 8.3 fusion.117
  604.4 8.4 fusion.115
  628.9 8.3 fusion.113
  639.3 9.2 %fusion.111 = (f32[3]{0:T(128)}, f32[3]{0:T(128)}, f32[3]{0:T(128)}, f32[3]{0:T(128)}, f32[3]{0:T(128)}, /*index=5*/f32[3]{0:T(128)}, f32[3]{0:T(128)}, f32[3]{0:T(128)}) fusion(f32[4096]{0:T(1024)} %get-tuple-element.147, f32[4096,3,64]{0,2,1:T(8,128)S(1)} %copy-done.2, bf16[4096,3,64]{0,2,1:T(8,128)(2,1)} %bitcast.320, pred[4096]{0:T(1024)(128)(4,1)S(1)} %copy-done.91, ...), kind=kLoop, calls=%fused_computation.179 | loop fusion | flops 20447208 | bytes 4853856 | tf_op jit(solution)/shard_map/reduce_sum | solution.py:251
  656.3 209.2 %all-reduce.43 = (f32[3,33]{1,0:T(4,128)}, f32[768]{0:T(1024)}, f32[768]{0:T(1024)}, f32[768,768]{1,0:T(8,128)}, f32[768,768]{1,0:T(8,128)}, /*index=5*/f32[768]{0:T(1024)}, f32[768]{0:T(1024)}) all-reduce(f32[3,33]{1,0:T(4,128)S(1)} %stack.135, f32[768]{0:T(1024)} %get-tuple-element.110, ...), channel_id=1, replica_groups=mesh['batch'=8,'head'=4] {'batch'}, use_global_device_ids=true, to_apply=%region_60.61 | all-reduce | flops 1182819 | bytes 7103256 | tf_op jit(solution)/shard_map/psum | solution.py:284
  (535 shorter events, 199.4 us)
Async XLA Ops:
  7.2 172.6 %copy-start = (bf16[192,768]{1,0:T(8,128)(2,1)S(1)}, bf16[192,768]{1,0:T(8,128)(2,1)}, u32[]{:S(2)}) copy-start(bf16[192,768]{1,0:T(8,128)(2,1)} %param.23) | copy-start | bytes 884740
  7.2 51.5 %copy-start.107 = (bf16[768,192]{0,1:T(8,128)(2,1)S(1)}, bf16[768,192]{0,1:T(8,128)(2,1)}, u32[]{:S(2)}) copy-start(bf16[768,192]{0,1:T(8,128)(2,1)} %param.20) | copy-start | bytes 884740
  7.2 51.5 %all-gather.3.cloned.1.call-start = ((), (), s32[]{:S(2)}) async-start(), calls=%async_computation.4 | async-start | bytes 7864320 | tf_op jit(solution)/shard_map/all_gather | solution.py:72
  8.0 236.4 %reduce-scatter.5.cloned.1.call-start = ((), (), s32[]{:S(2)}) async-start(), calls=%async_computation.5 | async-start | bytes 7864320 | tf_op jit(solution)/shard_map/reduce_scatter | solution.py:157
  10.6 88.6 %copy-start.44 = (f32[64,64]{1,0:T(8,128)}, f32[64,64]{1,0:T(8,128)S(1)}, u32[]{:S(2)}) copy-start(f32[64,64]{1,0:T(8,128)S(1)} %get-tuple-element.173) | copy-start | bytes 49156
  11.4 56.1 %copy-start.90 = (pred[4096]{0:T(1024)(128)(4,1)}, pred[4096]{0:T(1024)(128)(4,1)S(1)}, u32[]{:S(2)}) copy-start(pred[4096]{0:T(1024)(128)(4,1)S(1)} %get-tuple-element.117) | copy-start | bytes 12292
  11.4 134.1 %copy-start.99 = (f32[4096]{0:T(1024)}, f32[4096]{0:T(1024)S(1)}, u32[]{:S(2)}) copy-start(f32[4096]{0:T(1024)S(1)} %get-tuple-element.116) | copy-start | bytes 49156
  12.1 55.3 %copy-start.96 = (s32[4096]{0:T(1024)}, s32[4096]{0:T(1024)S(1)}, u32[]{:S(2)}) copy-start(s32[4096]{0:T(1024)S(1)} %multiply_add_fusion.1) | copy-start | bytes 49156
  13.6 55.3 %copy-start.120 = (f32[256]{0:T(256)}, f32[256]{0:T(256)S(1)}, u32[]{:S(2)}) copy-start(f32[256]{0:T(256)S(1)} %convert_reduce_fusion.1) | copy-start | bytes 3076
  24.0 77.7 %copy-start.4 = (pred[256,4096]{1,0:T(8,128)(4,1)}, pred[256,4096]{1,0:T(8,128)(4,1)S(1)}, u32[]{:S(2)}) copy-start(pred[256,4096]{1,0:T(8,128)(4,1)S(1)} %compare_and_fusion) | copy-start | bytes 3145732
  68.9 61.3 %copy-start.75 = (bf16[256,3,64]{0,2,1:T(8,128)(2,1)}, bf16[256,3,64]{0,2,1:T(8,128)(2,1)S(1)}, u32[]{:S(2)}) copy-start(bf16[256,3,64]{0,2,1:T(8,128)(2,1)S(1)} %get-tuple-element.151) | copy-start | bytes 294916
  144.9 34.8 %copy-start.92 = (f32[3,4096]{1,0:T(4,128)}, f32[3,4096]{1,0:T(4,128)S(1)}, u32[]{:S(2)}) copy-start(f32[3,4096]{1,0:T(4,128)S(1)} %log_add_fusion) | copy-start | bytes 147460
  185.8 58.5 %copy-start.6 = (bf16[1024,768]{1,0:T(8,128)(2,1)S(1)}, bf16[1024,768]{1,0:T(8,128)(2,1)}, u32[]{:S(2)}) copy-start(bf16[1024,768]{1,0:T(8,128)(2,1)} %param.16) | copy-start | bytes 4718596
  185.8 61.3 %copy-start.122 = (f32[768]{0:T(1024)S(1)}, f32[768]{0:T(1024)}, u32[]{:S(2)}) copy-start(f32[768]{0:T(1024)} %param.25) | copy-start | bytes 9220
  185.8 61.3 %copy-start.141 = (f32[768]{0:T(1024)S(1)}, f32[768]{0:T(1024)}, u32[]{:S(2)}) copy-start(f32[768]{0:T(1024)} %param.26) | copy-start | bytes 9220
  185.8 190.7 %all-gather.5.cloned.1.call-start = ((), (), s32[]{:S(2)}) async-start(), calls=%async_computation.6 | async-start | bytes 7864320 | tf_op jit(solution)/shard_map/all_gather | solution.py:197
  244.3 40.4 %slice-start.13 = ((s8[4718592]{0:T(1024)(128)(4,1)}), s8[4194304]{0:T(1024)(128)(4,1)S(1)}, s32[]{:S(2)}) async-start(s8[4718592]{0:T(1024)(128)(4,1)} %bitcast.394), calls=%async_computation.24 | async-start | bytes 8388608
  246.4 119.6 %copy-start.112 = (f32[1024]{0:T(1024)}, f32[1024]{0:T(1024)S(1)}, u32[]{:S(2)}) copy-start(f32[1024]{0:T(1024)S(1)} %broadcast_multiply_fusion.5) | copy-start | bytes 12292
  247.2 118.8 %copy-start.114 = (f32[1024]{0:T(1024)}, f32[1024]{0:T(1024)S(1)}, u32[]{:S(2)}) copy-start(f32[1024]{0:T(1024)S(1)} %add_rsqrt_fusion.1) | copy-start | bytes 12292
  247.2 37.5 %slice-start.14 = ((s8[4718592]{0:T(1024)(128)(4,1)}), s8[524288]{0:T(1024)(128)(4,1)S(1)}, s32[]{:S(2)}) async-start(s8[4718592]{0:T(1024)(128)(4,1)} %bitcast.394), calls=%async_computation.25 | async-start | bytes 1048576
  329.8 326.4 %reduce-scatter.11.cloned.1.call-start = ((), (), s32[]{:S(2)}) async-start(), calls=%async_computation.9 | async-start | bytes 5898240 | tf_op jit(solution)/shard_map/reduce_scatter | solution.py:193
  342.0 314.2 %reduce-scatter.9.cloned.1.call-start = ((), (), s32[]{:S(2)}) async-start(), calls=%async_computation.8 | async-start | bytes 5898240 | tf_op jit(solution)/shard_map/reduce_scatter | solution.py:190
  376.3 489.2 %reduce-scatter.7.cloned.1.call-start = ((), (), s32[]{:S(2)}) async-start(), calls=%async_computation.7 | async-start | bytes 7864320 | tf_op jit(solution)/shard_map/reduce_scatter | solution.py:274
  383.1 128.3 %copy-start.3 = (bf16[4096,192]{0,1:T(8,128)(2,1)}, bf16[4096,192]{0,1:T(8,128)(2,1)S(1)}, u32[]{:S(2)}) copy-start(bf16[4096,192]{0,1:T(8,128)(2,1)S(1)} %get-tuple-element.172) | copy-start | bytes 4718596
  511.4 59.8 %copy-start.104 = (bf16[768,192]{0,1:T(8,128)(2,1)S(1)}, bf16[768,192]{0,1:T(8,128)(2,1)}, u32[]{:S(2)}) copy-start(bf16[768,192]{0,1:T(8,128)(2,1)} %param.22) | copy-start | bytes 884740
  583.7 286.3 %all-reduce.42.cloned.1.call-start = ((), (), s32[]{:S(2)}) async-start(), calls=%async_computation.10 | async-start | bytes 4718592 | tf_op jit(solution)/shard_map/psum | solution.py:284
  639.3 226.2 %copy-start.113 = (f32[1024]{0:T(1024)S(1)}, f32[1024]{0:T(1024)}, u32[]{:S(2)}) copy-start(f32[1024]{0:T(1024)} %copy-done.112) | copy-start | bytes 12292
  639.3 226.2 %copy-start.115 = (f32[1024]{0:T(1024)S(1)}, f32[1024]{0:T(1024)}, u32[]{:S(2)}) copy-start(f32[1024]{0:T(1024)} %copy-done.114) | copy-start | bytes 12292
  639.3 226.2 %copy-start.117 = (f32[1024]{0:T(1024)S(1)}, f32[1024]{0:T(1024)}, u32[]{:S(2)}) copy-start(f32[1024]{0:T(1024)} %copy-done.116) | copy-start | bytes 12292
  639.3 226.2 %copy-start.119 = (f32[1024]{0:T(1024)S(1)}, f32[1024]{0:T(1024)}, u32[]{:S(2)}) copy-start(f32[1024]{0:T(1024)} %copy-done.118) | copy-start | bytes 12292
  639.3 226.2 %copy-start.123 = (f32[768]{0:T(1024)S(1)}, f32[768]{0:T(1024)}, u32[]{:S(2)}) copy-start(f32[768]{0:T(1024)} %param.25) | copy-start | bytes 9220
  648.5 217.0 %copy-start.7 = (bf16[1024,768]{1,0:T(8,128)(2,1)S(1)}, bf16[1024,768]{1,0:T(8,128)(2,1)}, u32[]{:S(2)}) copy-start(bf16[1024,768]{1,0:T(8,128)(2,1)} %param.16) | copy-start | bytes 4718596
  (133 other events, 853.6 us)
Sparse Core Ops, SparseCore 0:
  9.6 49.0 all-gather.2
  185.9 58.3 reduce-scatter.4
  330.0 46.4 all-gather.4
  379.0 47.8 reduce-scatter.10
  429.3 47.8 reduce-scatter.8
  583.8 58.8 reduce-scatter.6
  647.1 170.6 all-reduce.41
